TPU v7x, 32 devices: a whole 2x2x4 slice. The times are simulated.
32 devices in a mesh: orb: 16 (over z, y, core), slab: 2 (over x).
Axes of the slice: x: 2, y: 2, z: 4, core: 2. Of those that a mesh axis runs over, the one named last changes fastest.
Arguments:
- orbitals: bfloat16 [512, 8192], P('orb', 'slab'), may hold values from -6 to 6
- eigenpotentials: bfloat16 [1024, 8192], P(None, 'slab'), may hold values from -0.0625 to 0.0625
- screening: float32 [1024], replicated, may hold values from 0.02 to 2
- trial_vectors: bfloat16 [16, 16384], P(None, 'orb'), may hold values from -0.0029296875 to 0.0029296875
- pair_index: int32 [2, 16384], P(None, 'orb'), may hold values from -1 to 511, as said below
Outputs:
- direct: float32 [16, 16384], P(None, 'orb')
Inputs may be any that keep to these rules, and one draw needn't show every extreme that they name: `pair_index`: each column is a pair (i, j) of two different orbitals, or holds -1 in both rows for an empty slot. The 1024 slots of one pair owner (one device of orb) hold its pairs; in every draw some owner has all of its slots used.
All inputs are finite; a program needn't handle non-finite values.
Results may differ from a plain program's by a relative error of at most 0.0091.
Values may be sent and summed in bfloat16 or wider, within the bound.
A program may use at most 128 MiB of HBM per device.

v0:
```python
import jax
import jax.numpy as jnp
from jax import lax
from jax.sharding import PartitionSpec as P


def split_pair(matrix_in):
    upper_part = matrix_in.astype(jnp.bfloat16)
    lower_part = (matrix_in - upper_part.astype(jnp.float32)).astype(jnp.bfloat16)
    return jnp.concatenate([upper_part, lower_part], 0)


def fold_halves(stacked):
    half_rows = stacked.shape[0] // 2
    return stacked[:half_rows] + stacked[half_rows:]


def contract_last(left_side, right_side):
    return lax.dot_general(
        left_side, right_side, (((1,), (1,)), ((), ())), preferred_element_type=jnp.float32
    )


def project_trials(trial_vectors, coef_split):
    return fold_halves(contract_last(coef_split, trial_vectors)).T


def apply_screened(scaled, coef_split):
    half_rows = coef_split.shape[0] // 2
    upper_coef = coef_split[:half_rows]
    lower_coef = coef_split[half_rows:]
    scaled_split = split_pair(scaled)
    main_part = fold_halves(jnp.dot(scaled_split, upper_coef, preferred_element_type=jnp.float32))
    scaled_rows = scaled_split[: scaled.shape[0]]
    return main_part + jnp.dot(scaled_rows, lower_coef, preferred_element_type=jnp.float32)


def shards(orbitals, eigenpotentials, screening, trial_vectors, pair_index):
    gathered = lax.all_gather(orbitals, "orb", axis=0, tiled=True)
    is_live = pair_index[0] >= 0
    first_rows = jnp.take(gathered, jnp.maximum(pair_index[0], 0), axis=0)
    second_rows = jnp.take(gathered, jnp.maximum(pair_index[1], 0), axis=0)
    density = jnp.where(is_live[:, None], first_rows * second_rows, jnp.zeros((), jnp.bfloat16))
    share_rows = eigenpotentials.shape[0] // lax.axis_size("slab")
    shares = lax.psum_scatter(
        contract_last(eigenpotentials, density), "slab", scatter_dimension=0, tiled=True
    )
    share_scale = lax.dynamic_slice_in_dim(
        screening, lax.axis_index("slab") * share_rows, share_rows, 0
    )
    share_split = split_pair(shares)
    owner_terms = project_trials(trial_vectors, share_split)
    projected = lax.psum(owner_terms, "orb")
    slab_terms = apply_screened(projected * share_scale[None, :], share_split)
    direct = lax.psum(slab_terms, "slab")
    return direct


def solution(mesh):
    return jax.shard_map(
        shards,
        mesh=mesh,
        in_specs=(P("orb", "slab"), P(None, "slab"), P(), P(None, "orb"), P(None, "orb")),
        out_specs=P(None, "orb"),
        check_vma=False,
    )
```

profile of v0, /device:TPU:0, one launch (start us, length us, event | category | flops | bytes accessed | tf_op | source)
XLA Modules:
  0.0 259.0 jit_solution(12866672698695216599)
XLA Ops:
  6.5 0.0 copy-start
  6.5 0.0 all-gather.2.cloned.1.call-start
  6.5 0.7 all-gather.2.cloned.1.call-update
  7.3 0.0 reduce-scatter.2.cloned.1.call-start
  7.3 0.7 compare_reduce_fusion
  8.0 0.8 slice_maximum_fusion.1
  8.9 53.8 %all-gather.2.cloned.1.call-done = bf16[512,4096]{1,0:T(8,128)(2,1)} async-done(((bf16[32,4096]{1,0:T(8,128)(2,1)}), bf16[512,4096]{1,0:T(8,128)(2,1)}) %all-gather.2.cloned.1.call-update) | async-done | bytes 4194320 | tf_op jit(solution)/shard_map/all_gather | solution.py:39
  62.6 17.8 %gather_fusion = bf16[1024,4096]{1,0:T(8,128)(2,1)} fusion(bf16[512,4096]{1,0:T(8,128)(2,1)} %all-gather.2.cloned.1.call-done, s32[1024]{0:T(1024)S(1)} %fusion.21), kind=kCustom, calls=%fused_computation.clone | custom fusion | bytes 16781312 | tf_op jit(solution)/shard_map/jit(_take)/gather | solution.py:41
  80.4 17.8 %gather_fusion.1 = bf16[1024,4096]{1,0:T(8,128)(2,1)} fusion(bf16[512,4096]{1,0:T(8,128)(2,1)} %all-gather.2.cloned.1.call-done, s32[1024]{0:T(1024)S(1)} %fusion.22), kind=kCustom, calls=%fused_computation.1.clone | custom fusion | bytes 16781312 | tf_op jit(solution)/shard_map/jit(_take)/gather | solution.py:42
  98.2 0.0 copy-start.1
  98.2 16.6 %fusion.9 = f32[1024,1024]{0,1:T(8,128)} fusion(bf16[1024,4096]{1,0:T(8,128)(2,1)} %param.8, bf16[1024,4096]{1,0:T(8,128)(2,1)} %gather_fusion.1, bf16[1024,4096]{1,0:T(8,128)(2,1)} %gather_fusion, pred[1024]{0:T(1024)(128)(4,1)S(1)} %get-tuple-element.12, pred[1024]{0:T(1024)(128)(4,1)S(1)} %get-tuple-element.13, pred[1024]{0:T(1024)(128)(4,1)S(1)} %compare_reduce_fusion), kind=kOutput, calls=%fused_computation.11 | convolution fusion | flops 8606711808 | bytes 29363200 | tf_op jit(solution)/shard_map/dot_general | solution.py:19
  114.8 0.0 reduce-scatter.2.cloned.1.call-update
  114.9 0.0 all-reduce.2.cloned.1.call-start
  114.9 0.0 copy-done.1
  114.9 0.1 dynamic_slice.3
  115.0 52.9 %reduce-scatter.2.cloned.1.call-done = f32[512,1024]{0,1:T(8,128)} async-done(((f32[1024,1024]{0,1:T(8,128)}), f32[512,1024]{0,1:T(8,128)}) %reduce-scatter.2.cloned.1.call-update) | async-done | bytes 2097168 | tf_op jit(solution)/shard_map/reduce_scatter | solution.py:45
  167.9 2.8 %subtract_convert_fusion = (bf16[512,1024]{0,1:T(8,128)(2,1)S(1)}, bf16[512,1024]{0,1:T(8,128)(2,1)S(1)}) fusion(f32[512,1024]{0,1:T(8,128)} %reduce-scatter.2.cloned.1.call-done), kind=kLoop, calls=%fused_computation.16 | loop fusion | flops 2097152 | bytes 4194304 | tf_op jit(solution)/shard_map/convert_element_type | solution.py:9
  170.7 0.0 copy-done
  170.7 0.4 fusion.12
  171.1 61.0 %psum.14 = f32[16,512]{1,0:T(8,128)S(1)} all-reduce(f32[16,512]{1,0:T(8,128)S(1)} %fusion.16), channel_id=1, replica_groups=mesh['orb'=16,'slab'=2] {'orb'}, use_global_device_ids=true, to_apply=%region_1.3 | all-reduce | flops 8192 | bytes 65536 | tf_op jit(solution)/shard_map/psum | solution.py:53
  232.2 0.4 fusion.17
  232.6 1.0 convolution_add_fusion
  233.6 0.0 all-reduce.2.cloned.1.call-update
  233.6 17.4 %all-reduce.2.cloned.1.call-done = f32[16,1024]{1,0:T(8,128)} async-done(((f32[16,1024]{1,0:T(8,128)}), f32[16,1024]{1,0:T(8,128)}) %all-reduce.2.cloned.1.call-update) | async-done | bytes 65552 | tf_op jit(solution)/shard_map/psum | solution.py:55
  251.0 1.5 copy.7
  (5 shorter events, 0.0 us)
Async XLA Ops:
  6.5 164.2 %copy-start = (bf16[16,1024]{1,0:T(8,128)(2,1)S(1)}, bf16[16,1024]{1,0:T(8,128)(2,1)}, u32[]{:S(2)}) copy-start(bf16[16,1024]{1,0:T(8,128)(2,1)} %param.10) | copy-start | bytes 98308
  6.5 56.1 %all-gather.2.cloned.1.call-start = ((), (), s32[]{:S(2)}) async-start(), calls=%async_computation.1 | async-start | bytes 4456448 | tf_op jit(solution)/shard_map/all_gather | solution.py:39
  7.3 160.6 %reduce-scatter.2.cloned.1.call-start = ((), (), s32[]{:S(2)}) async-start(), calls=%async_computation.2 | async-start | bytes 6291456 | tf_op jit(solution)/shard_map/reduce_scatter | solution.py:45
  98.2 16.7 %copy-start.1 = (f32[1024]{0:T(1024)S(1)}, f32[1024]{0:T(1024)}, u32[]{:S(2)}) copy-start(f32[1024]{0:T(1024)} %param.9) | copy-start | bytes 12292
  114.9 136.2 %all-reduce.2.cloned.1.call-start = ((), (), s32[]{:S(2)}) async-start(), calls=%async_computation.3 | async-start | bytes 131072 | tf_op jit(solution)/shard_map/psum | solution.py:55
Sparse Core Ops, SparseCore 0:
  9.5 53.0 all-gather.1
  115.0 52.8 reduce-scatter.1
  233.7 17.2 all-reduce.1
where the time goes:
time: 259 us
  waiting for transfers between devices  125 us (48%)
  blocking collectives  61 us (24%)
  local copies, waits for them, and re-layouts  37.2 us (14%)
  matrix products  18.4 us (7%)
  between operations  13.2 us (5%)
  other arithmetic  4.34 us (2%)
    psum x1, blocking collectives, shards(): projected = lax.psum(owner_terms, 'orb')  61 us
    all_gather x1, waiting for transfers between devices, shards(): gathered = lax.all_gather(orbitals, 'orb', axis=0, tiled=True)  53.8 us
    reduce_scatter x1, waiting for transfers between devices, shards(): lax.psum_scatter(contract_last(eigenpotentials, density), 'slab', scatter...  52.9 us
    gather x1, local copies, waits for them, and re-layouts, shards(): second_rows = jnp.take(gathered, jnp.maximum(pair_index[1], 0), axis=0)  17.8 us
    gather x1, local copies, waits for them, and re-layouts, shards(): first_rows = jnp.take(gathered, jnp.maximum(pair_index[0], 0), axis=0)  17.8 us
    psum x1, waiting for transfers between devices, shards(): direct = lax.psum(slab_terms, 'slab')  17.4 us
    dot_general x2, matrix products, contract_last(): lax.dot_general(left_side, right_side, (((1,), (1,)), ((), ())), preferre...  17 us
  transfers between devices with their start and end apart: 3, of which 3 were waited for; matrix products, arithmetic and copies ran while one was open for 1% of the time, Pallas kernels for 0%

commit v1 on v0

v1 whole, which is shorter than its diff:
```python
import functools

import jax
import jax.numpy as jnp
from jax import lax
from jax.experimental import pallas as pl
from jax.experimental.pallas import tpu as pltpu
from jax.sharding import PartitionSpec as P

QUAD = 4
LANES = 128
MESH_ID = pl.DeviceIdType.MESH
VMEM_SPEC = pl.BlockSpec(memory_space=pltpu.VMEM)
ANY_SPEC = pl.BlockSpec(memory_space=pl.ANY)


def greet(peers):
    barrier = pltpu.get_barrier_semaphore()
    for peer in peers:
        pl.semaphore_signal(barrier, inc=1, device_id=peer, device_id_type=MESH_ID)
    return lambda: pl.semaphore_wait(barrier, len(peers))


def columns(start, size):
    return pl.ds(pl.multiple_of(start * size, size), size)


def spread_kernel(
    groups, orb_ref, trial_ref, pair_ref, table_ref, trials_ref, pairs_ref,
    own_sem, a_send, a_recv, y_send, y_recv, c_send, c_recv, t_send, t_recv, p_send, p_recv,
):
    me = lax.axis_index("orb")
    group, place = me // QUAD, lax.rem(me, QUAD)
    core = place + 1 - 2 * lax.rem(place, 2)
    side = lax.rem(place + 2, QUAD)
    width = table_ref.shape[2]

    def device(g, q):
        return {"orb": g * QUAD + q}

    others = [lax.rem(group + k, groups) for k in range(1, groups)]
    sources = [lax.rem(group + groups - k, groups) for k in range(1, groups)]
    ready = greet(
        [device(g, place) for g in others] + [device(group, core), device(group, side)]
    )

    def out_block(g):
        return orb_ref.at[:, columns(g, width)]

    own = pltpu.make_async_copy(out_block(group), table_ref.at[me], own_sem.at[0])
    own_t = pltpu.make_async_copy(trial_ref, trials_ref.at[group], own_sem.at[1])
    own_p = pltpu.make_async_copy(pair_ref, pairs_ref.at[group], own_sem.at[2])
    for copy in (own, own_t, own_p):
        copy.start()

    def remote(src, dst, send, recv, target):
        return pltpu.make_async_remote_copy(
            src_ref=src, dst_ref=dst, send_sem=send, recv_sem=recv,
            device_id=target, device_id_type=MESH_ID,
        )

    def across(k, sender):
        g = others[k]
        return remote(
            out_block(g), table_ref.at[sender * QUAD + place],
            a_send.at[k], a_recv.at[sender], device(g, place),
        )

    def to_side(k, g, src, q):
        return remote(
            src, table_ref.at[g * QUAD + q], y_send.at[k], y_recv.at[k], device(group, side)
        )

    def to_core(k, g, src, q):
        return remote(
            src, table_ref.at[g * QUAD + q], c_send.at[k], c_recv.at[k], device(group, core)
        )

    def trial_copy(k, sender):
        return remote(
            trial_ref, trials_ref.at[sender], t_send.at[k], t_recv.at[sender],
            device(others[k], place),
        )

    def pair_copy(k, sender):
        return remote(
            pair_ref, pairs_ref.at[sender], p_send.at[k], p_recv.at[sender],
            device(others[k], place),
        )

    ready()
    sent = []

    def go(copy):
        copy.start()
        sent.append(copy)

    for k in range(groups - 1):
        go(across(k, group))
    go(to_side(0, group, out_block(group), place))
    go(to_core(0, group, out_block(group), place))
    for k in range(groups - 1):
        go(pair_copy(k, group))
        go(trial_copy(k, group))

    def relay(k):
        g = group if k == 0 else sources[k - 1]
        to_side(k, g, out_block(group), side).wait_recv()
        go(to_core(groups + k, g, table_ref.at[g * QUAD + side], side))

    for k in range(1, groups):
        g = sources[k - 1]
        across(k - 1, g).wait_recv()
        src = table_ref.at[g * QUAD + place]
        go(to_side(k, g, src, place))
        go(to_core(k, g, src, place))
        relay(k - 1)
    relay(groups - 1)
    far = lax.rem(core + 2, QUAD)
    for k in range(groups):
        g = group if k == 0 else sources[k - 1]
        to_core(k, g, out_block(group), core).wait_recv()
        to_core(groups + k, g, out_block(group), far).wait_recv()
    for k in range(groups - 1):
        trial_copy(k, sources[k]).wait_recv()
        pair_copy(k, sources[k]).wait_recv()
    for copy in sent:
        copy.wait_send()
    for copy in (own, own_t, own_p):
        copy.wait()


def spread(count, orbitals, trial_vectors, pair_index):
    groups = count // QUAD
    rows, grid_points = orbitals.shape
    width = grid_points // groups
    dma = pltpu.SemaphoreType.DMA
    return pl.pallas_call(
        functools.partial(spread_kernel, groups),
        out_shape=(
            jax.ShapeDtypeStruct((count, rows, width), orbitals.dtype),
            jax.ShapeDtypeStruct((groups, *trial_vectors.shape), trial_vectors.dtype),
            jax.ShapeDtypeStruct((groups, *pair_index.shape), pair_index.dtype),
        ),
        in_specs=[VMEM_SPEC] * 3,
        out_specs=(ANY_SPEC,) * 3,
        scratch_shapes=[
            dma((3,)), dma((groups,)), dma((groups,)), dma((groups,)), dma((groups,)),
            dma((2 * groups,)), dma((2 * groups,)),
            dma((groups,)), dma((groups,)), dma((groups,)), dma((groups,)),
        ],
        compiler_params=pltpu.CompilerParams(collective_id=0, has_side_effects=True),
    )(orbitals, trial_vectors, pair_index)


def density_kernel(pair_ref, trial_ref, table_ref, dens_ref, field_ref, turned):
    first_step = (pl.program_id(0) == 0) & (pl.program_id(1) == 0)

    @pl.when(first_step)
    def _():
        turned[...] = table_ref[...].T
        field_ref[...] = jnp.zeros_like(field_ref)

    index = pair_ref[0]
    is_live = jnp.max(index) >= 0

    @pl.when(is_live)
    def _():
        orbs = turned.shape[1]
        ids = lax.broadcasted_iota(jnp.int32, (orbs, index.shape[1]), 0)

        def pick(row):
            return jnp.where(ids == index[row : row + 1], 1.0, 0.0).astype(jnp.bfloat16)

        left, right = pick(0), pick(1)
        trial = trial_ref[0]
        step = min(512, turned.shape[0])
        for c in range(turned.shape[0] // step):
            rows = pl.ds(c * step, step)
            part = turned[rows, :]
            one = jnp.dot(part, left, preferred_element_type=jnp.float32)
            two = jnp.dot(part, right, preferred_element_type=jnp.float32)
            dens = (one * two).astype(jnp.bfloat16)
            dens_ref[rows, :] = dens
            field_ref[:, rows] += lax.dot_general(
                trial, dens, (((1,), (1,)), ((), ())), preferred_element_type=jnp.float32
            )

    @pl.when(jnp.logical_not(is_live))
    def _():
        dens_ref[...] = jnp.zeros_like(dens_ref)


def densities(pairs, trials, table):
    groups, batch, slots = trials.shape
    count, rows, width = table.shape
    orbs = count * rows
    block = min(512, slots)
    steps = slots // block
    return pl.pallas_call(
        density_kernel,
        grid=(groups, steps),
        out_shape=(
            jax.ShapeDtypeStruct((width, groups * slots), jnp.bfloat16),
            jax.ShapeDtypeStruct((batch, width), jnp.float32),
        ),
        in_specs=[
            pl.BlockSpec((1, 2, block), lambda g, i: (g, 0, i)),
            pl.BlockSpec((1, batch, block), lambda g, i: (g, 0, i)),
            pl.BlockSpec((orbs, width), lambda g, i: (0, 0)),
        ],
        out_specs=(
            pl.BlockSpec((width, block), lambda g, i: (0, g * steps + i)),
            pl.BlockSpec((batch, width), lambda g, i: (0, 0)),
        ),
        scratch_shapes=[pltpu.VMEM((width, orbs), jnp.bfloat16)],
    )(pairs, trials, table.reshape(orbs, width))


def split_rows(values):
    upper = values.astype(jnp.bfloat16)
    lower = (values - upper.astype(jnp.float32)).astype(jnp.bfloat16)
    return jnp.concatenate([upper, lower], 0)


def fold(stacked):
    half = stacked.shape[0] // 2
    return stacked[:half] + stacked[half:]


def apply_kernel(
    count, slabs, field_ref, scale_ref, eig_ref, dens_ref, out_ref,
    eig, dens, pieces, rs_in, slab_in, gathered, screened, potential, shares, share_in, slab_out,
    load_sem, rs_send, rs_recv, sl_send, sl_recv, ag_send, ag_recv, d_send, d_recv, o_send, o_recv,
):
    me, slab = lax.axis_index("orb"), lax.axis_index("slab")
    groups = count // QUAD
    group, place = me // QUAD, lax.rem(me, QUAD)
    batch, width = field_ref.shape
    slots = out_ref.shape[1]
    tall = pieces.shape[1]
    bands = batch // tall
    ranks = [lax.rem(me + k, count) for k in range(1, count)]
    origins = [lax.rem(me + count - k, count) for k in range(1, count)]
    layers = [lax.rem(slab + k, slabs) for k in range(1, slabs)]
    layer_from = [lax.rem(slab + slabs - k, slabs) for k in range(1, slabs)]
    ready = greet([{"orb": r} for r in ranks] + [{"slab": s} for s in layers])

    load = pltpu.make_async_copy(eig_ref.at[:, columns(group, width)], eig, load_sem.at[0])
    load.start()
    dens_loads = [
        pltpu.make_async_copy(
            dens_ref.at[:, pl.ds(g * slots, slots)], dens.at[g], load_sem.at[1 + g]
        )
        for g in range(groups)
    ]
    for copy in dens_loads:
        copy.start()

    def remote(src, dst, send, recv, target):
        return pltpu.make_async_remote_copy(
            src_ref=src, dst_ref=dst, send_sem=send, recv_sem=recv,
            device_id=target, device_id_type=MESH_ID,
        )

    sent = []

    def go(copy):
        copy.start()
        sent.append(copy)

    field = split_rows(field_ref[...])
    load.wait()
    for c in range(eig.shape[0] // LANES):
        part = fold(
            lax.dot_general(
                field, eig[pl.ds(c * LANES, LANES), :], (((1,), (1,)), ((), ())),
                preferred_element_type=jnp.float32,
            )
        )
        for h in range(bands):
            pieces[c * bands + h] = part[h * tall : (h + 1) * tall]

    def scatter(k, sender):
        return remote(
            pieces.at[ranks[k]], rs_in.at[sender], rs_send.at[k], rs_recv.at[sender],
            {"orb": ranks[k]},
        )

    def layer_copy(k, sender):
        return remote(
            slab_in.at[sender], slab_in.at[sender], sl_send.at[k], sl_recv.at[sender],
            {"slab": layers[k]},
        )

    def gather(k, sender):
        return remote(
            gathered.at[sender], gathered.at[sender], ag_send.at[k], ag_recv.at[sender],
            {"orb": ranks[k]},
        )

    ready()
    for k in range(count - 1):
        go(scatter(k, me))
    total = pieces[me]
    for k in range(count - 1):
        scatter(k, origins[k]).wait_recv()
        total = total + rs_in[origins[k]]
    slab_in[slab] = total
    for k in range(slabs - 1):
        go(layer_copy(k, slab))
    for k in range(slabs - 1):
        layer_copy(k, layer_from[k]).wait_recv()
    total = slab_in[0]
    for s in range(1, slabs):
        total = total + slab_in[s]
    gathered[me] = total
    for k in range(count - 1):
        go(gather(k, me))
    for k in range(count - 1):
        gather(k, origins[k]).wait_recv()
    for c in range(count // bands):
        rows = jnp.concatenate([gathered[c * bands + h] for h in range(bands)], 0)
        cols = slice(c * LANES, (c + 1) * LANES)
        screened[:, cols] = split_rows(rows * scale_ref[:, cols])

    for c in range(width // 256):
        cols = pl.ds(c * 256, 256)
        potential[:, cols] = split_rows(
            fold(jnp.dot(screened[...], eig[:, cols], preferred_element_type=jnp.float32))
        )

    for copy in dens_loads:
        copy.wait()

    def apply_to(g):
        @pl.loop(0, slots // 256)
        def _(c):
            cols = columns(c, 256)
            shares[g, :, cols] = fold(
                jnp.dot(potential[...], dens[g, :, cols], preferred_element_type=jnp.float32)
            )

    goals = [lax.rem(group + k, groups) for k in range(1, groups)]
    givers = [lax.rem(group + groups - k, groups) for k in range(1, groups)]

    def share_copy(k, sender):
        return remote(
            shares.at[goals[k]], share_in.at[sender], d_send.at[k], d_recv.at[sender],
            {"orb": goals[k] * QUAD + place},
        )

    def out_copy(k, sender):
        return remote(
            slab_out.at[sender], slab_out.at[sender], o_send.at[k], o_recv.at[sender],
            {"slab": layers[k]},
        )

    for k in range(groups - 1):
        apply_to(goals[k])
        go(share_copy(k, group))
    apply_to(group)
    total = shares[group]
    for k in range(groups - 1):
        share_copy(k, givers[k]).wait_recv()
        total = total + share_in[givers[k]]
    slab_out[slab] = total
    for k in range(slabs - 1):
        go(out_copy(k, slab))
    for k in range(slabs - 1):
        out_copy(k, layer_from[k]).wait_recv()
    total = slab_out[0]
    for s in range(1, slabs):
        total = total + slab_out[s]
    out_ref[...] = total
    for copy in sent:
        copy.wait_send()


def apply_direct(count, slabs, field, screening, eigenpotentials, dens, slots):
    groups = count // QUAD
    batch, width = field.shape
    neig = eigenpotentials.shape[0]
    tall = batch * neig // (count * LANES)
    dma = pltpu.SemaphoreType.DMA
    f32, b16 = jnp.float32, jnp.bfloat16
    return pl.pallas_call(
        functools.partial(apply_kernel, count, slabs),
        out_shape=jax.ShapeDtypeStruct((batch, slots), f32),
        in_specs=[VMEM_SPEC, VMEM_SPEC, ANY_SPEC, ANY_SPEC],
        out_specs=VMEM_SPEC,
        scratch_shapes=[
            pltpu.VMEM((neig, width), b16),
            pltpu.VMEM((groups, width, slots), b16),
            pltpu.VMEM((count, tall, LANES), f32),
            pltpu.VMEM((count, tall, LANES), f32),
            pltpu.VMEM((slabs, tall, LANES), f32),
            pltpu.VMEM((count, tall, LANES), f32),
            pltpu.VMEM((2 * batch, neig), b16),
            pltpu.VMEM((2 * batch, width), b16),
            pltpu.VMEM((groups, batch, slots), f32),
            pltpu.VMEM((groups, batch, slots), f32),
            pltpu.VMEM((slabs, batch, slots), f32),
            dma((1 + groups,)),
            dma((count,)), dma((count,)), dma((slabs,)), dma((slabs,)),
            dma((count,)), dma((count,)), dma((groups,)), dma((groups,)),
            dma((slabs,)), dma((slabs,)),
        ],
        compiler_params=pltpu.CompilerParams(collective_id=1, has_side_effects=True),
    )(field, screening.reshape(1, neig), eigenpotentials, dens)


def shards(count, slabs, orbitals, eigenpotentials, screening, trial_vectors, pair_index):
    table, trials, pairs = spread(count, orbitals, trial_vectors, pair_index)
    dens, field = densities(pairs, trials, table)
    slots = trial_vectors.shape[1]
    return apply_direct(count, slabs, field, screening, eigenpotentials, dens, slots)


def solution(mesh):
    return jax.shard_map(
        functools.partial(shards, mesh.shape["orb"], mesh.shape["slab"]),
        mesh=mesh,
        in_specs=(P("orb", "slab"), P(None, "slab"), P(), P(None, "orb"), P(None, "orb")),
        out_specs=P(None, "orb"),
        check_vma=False,
    )
```

time: 259 us -> 65.4 us (0.25)
  waiting for transfers between devices: 125 us -> 0 us
  Pallas kernels: 0 us -> 63.7 us
  blocking collectives: 61 us -> 0 us
  local copies, waits for them, and re-layouts: 37.2 us -> 1.47 us
  matrix products: 18.4 us -> 0 us
  between operations: 13.2 us -> 0.02 us
  other arithmetic: 4.34 us -> 0 us
    pallas_call x0 -> x3, Pallas kernels: none -> 63.7 us  [the longest x1 30.2 us: apply_direct(): pl.pallas_call(functools.partial(apply_kernel, count, slabs), out_shape=j...]
    psum x1 -> x0, blocking collectives: 61 us -> none  [shards(): projected = lax.psum(owner_terms, 'orb')]
    all_gather x1 -> x0, waiting for transfers between devices: 53.8 us -> none  [shards(): gathered = lax.all_gather(orbitals, 'orb', axis=0, tiled=True)]
    reduce_scatter x1 -> x0, waiting for transfers between devices: 52.9 us -> none  [shards(): lax.psum_scatter(contract_last(eigenpotentials, density), 'slab', scatter...]
    gather x2 -> x0, local copies, waits for them, and re-layouts: 35.6 us -> none  [the longest x1 17.8 us: shards(): second_rows = jnp.take(gathered, jnp.maximum(pair_index[1], 0), axis=0)]
    dot_general x4 -> x0, matrix products: 18.4 us -> none  [the longest x2 17 us: contract_last(): lax.dot_general(left_side, right_side, (((1,), (1,)), ((), ())), preferre...]
    psum x1 -> x0, waiting for transfers between devices: 17.4 us -> none  [shards(): direct = lax.psum(slab_terms, 'slab')]
    convert_element_type x2 -> x0, other arithmetic: 2.81 us -> none  [split_pair(): (matrix_in - upper_part.astype(jnp.float32)).astype(jnp.bfloat16)]
  transfers between devices with their start and end apart: 3 -> 0, of which waited for: 3 -> 0; matrix products, arithmetic and copies ran while one was open for 1% -> 0% of each run, Pallas kernels for 0% -> 0%
where the time goes in v1:
time: 65.4 us; the launch traced here: 65.2 us
  Pallas kernels  63.7 us (97%)
  local copies, waits for them, and re-layouts  1.47 us (2%)
    pallas_call x1, Pallas kernels, apply_direct(): pl.pallas_call(functools.partial(apply_kernel, count, slabs), out_shape=j...  30.2 us
    pallas_call x1, Pallas kernels, spread(): pl.pallas_call(functools.partial(spread_kernel, groups), out_shape=(jax.S...  19.6 us
    pallas_call x1, Pallas kernels, densities(): pl.pallas_call(density_kernel, grid=(groups, steps), out_shape=(jax.Shape...  13.9 us
    unnamed x1, local copies, waits for them, and re-layouts  1.47 us

profile of v1, /device:TPU:0, one launch (start us, length us, event | category | flops | bytes accessed | tf_op | source)
XLA Modules:
  0.0 65.2 jit_solution(611398928924694672)
XLA Ops:
  0.0 19.6 %shard_map.55 = (bf16[16,32,1024]{2,1,0:T(8,128)(2,1)}, bf16[4,16,1024]{2,1,0:T(8,128)(2,1)}, s32[4,2,1024]{2,1,0:T(2,128)}) custom-call(bf16[32,4096]{1,0:T(8,128)(2,1)} %orb_ref.1, bf16[16,1024]{1,0:T(8,128)(2,1)} %trial_ref.1, s32[2,1024]{1,0:T(2,128)} %pair_ref.1), custom_call_target="tpu_custom_call" | custom-call | tf_op jit(solution)/shard_map/pallas_call | solution.py:138
  19.6 13.9 %shard_map.56 = (bf16[1024,4096]{1,0:T(8,128)(2,1)}, f32[16,1024]{1,0:T(8,128)}) custom-call(s32[4,2,1024]{2,1,0:T(2,128)} %get-tuple-element.10.pair_ref, bf16[4,16,1024]{2,1,0:T(8,128)(2,1)} %get-tuple-element.11.trial_ref, bf16[512,1024]{1,0:T(8,128)(2,1)} %bitcast.2), custom_call_target="tpu_custom_call" | custom-call | tf_op jit(solution)/shard_map/pallas_call | solution.py:200
  33.5 30.2 %shard_map.57 = f32[16,1024]{1,0:T(8,128)} custom-call(f32[16,1024]{1,0:T(8,128)} %get-tuple-element.13.field_ref, f32[1,1024]{1,0:T(1,128)} %bitcast.3, bf16[1024,4096]{1,0:T(8,128)(2,1)} %eig_ref.1, bf16[1024,4096]{1,0:T(8,128)(2,1)} %get-tuple-element.14.dens_ref), custom_call_target="tpu_custom_call" | custom-call | tf_op jit(solution)/shard_map/pallas_call | solution.py:387
  63.7 1.5 %copy.7 = f32[16,1024]{1,0:T(8,128)} copy(f32[16,1024]{1,0:T(8,128)} %shard_map.57) | data formatting | bytes 131072

commit v2 on v1

--- a/solution.py
+++ b/solution.py
@@ -26,10 +26,13 @@
 
 
 def spread_kernel(
-    groups, orb_ref, trial_ref, pair_ref, table_ref, trials_ref, pairs_ref,
+    groups, slabs, orb_hbm, trial_ref, pair_ref, table_ref, trials_ref, pairs_ref, orb_ref,
     own_sem, a_send, a_recv, y_send, y_recv, c_send, c_recv, t_send, t_recv, p_send, p_recv,
+    r_send, r_recv,
 ):
-    me = lax.axis_index("orb")
+    me, slab = lax.axis_index("orb"), lax.axis_index("slab")
+    stage = pltpu.make_async_copy(orb_hbm, orb_ref, own_sem.at[3])
+    stage.start()
     group, place = me // QUAD, lax.rem(me, QUAD)
     core = place + 1 - 2 * lax.rem(place, 2)
     side = lax.rem(place + 2, QUAD)
@@ -40,8 +43,12 @@
 
     others = [lax.rem(group + k, groups) for k in range(1, groups)]
     sources = [lax.rem(group + groups - k, groups) for k in range(1, groups)]
+    layers = [lax.rem(slab + k, slabs) for k in range(1, slabs)]
+    layer_from = [lax.rem(slab + slabs - k, slabs) for k in range(1, slabs)]
     ready = greet(
-        [device(g, place) for g in others] + [device(group, core), device(group, side)]
+        [device(g, place) for g in others]
+        + [device(group, core), device(group, side)]
+        + [{"slab": x} for x in layers]
     )
 
     def out_block(g):
@@ -50,8 +57,8 @@
     own = pltpu.make_async_copy(out_block(group), table_ref.at[me], own_sem.at[0])
     own_t = pltpu.make_async_copy(trial_ref, trials_ref.at[group], own_sem.at[1])
     own_p = pltpu.make_async_copy(pair_ref, pairs_ref.at[group], own_sem.at[2])
-    for copy in (own, own_t, own_p):
-        copy.start()
+    own_t.start()
+    own_p.start()
 
     def remote(src, dst, send, recv, target):
         return pltpu.make_async_remote_copy(
@@ -78,9 +85,14 @@
 
     def trial_copy(k, sender):
         return remote(
-            trial_ref, trials_ref.at[sender], t_send.at[k], t_recv.at[sender],
+            trial_ref.at[slab], trials_ref.at[sender, slab], t_send.at[k], t_recv.at[sender],
             device(others[k], place),
         )
+
+    def trial_relay(k, n, owner):
+        part = trials_ref.at[sources[k], owner]
+        slot = k * slabs + n
+        return remote(part, part, r_send.at[slot], r_recv.at[slot], {"slab": layers[n]})
 
     def pair_copy(k, sender):
         return remote(
@@ -88,6 +100,7 @@
             device(others[k], place),
         )
 
+    stage.wait()
     ready()
     sent = []
 
@@ -103,6 +116,8 @@
         go(pair_copy(k, group))
         go(trial_copy(k, group))
 
+    own.start()
+
     def relay(k):
         g = group if k == 0 else sources[k - 1]
         to_side(k, g, out_block(group), side).wait_recv()
@@ -115,6 +130,10 @@
         go(to_side(k, g, src, place))
         go(to_core(k, g, src, place))
         relay(k - 1)
+    for k in range(groups - 1):
+        trial_copy(k, sources[k]).wait_recv()
+        for n in range(slabs - 1):
+            go(trial_relay(k, n, slab))
     relay(groups - 1)
     far = lax.rem(core + 2, QUAD)
     for k in range(groups):
@@ -122,35 +141,41 @@
         to_core(k, g, out_block(group), core).wait_recv()
         to_core(groups + k, g, out_block(group), far).wait_recv()
     for k in range(groups - 1):
-        trial_copy(k, sources[k]).wait_recv()
         pair_copy(k, sources[k]).wait_recv()
+        for n in range(slabs - 1):
+            trial_relay(k, n, layer_from[n]).wait_recv()
     for copy in sent:
         copy.wait_send()
     for copy in (own, own_t, own_p):
         copy.wait()
 
 
-def spread(count, orbitals, trial_vectors, pair_index):
+def spread(count, slabs, orbitals, trial_vectors, pair_index):
     groups = count // QUAD
+    batch, slots = trial_vectors.shape
+    parts = trial_vectors.reshape(slabs, batch // slabs, slots)
     rows, grid_points = orbitals.shape
     width = grid_points // groups
     dma = pltpu.SemaphoreType.DMA
-    return pl.pallas_call(
-        functools.partial(spread_kernel, groups),
+    table, trials, pairs = pl.pallas_call(
+        functools.partial(spread_kernel, groups, slabs),
         out_shape=(
             jax.ShapeDtypeStruct((count, rows, width), orbitals.dtype),
-            jax.ShapeDtypeStruct((groups, *trial_vectors.shape), trial_vectors.dtype),
+            jax.ShapeDtypeStruct((groups, *parts.shape), parts.dtype),
             jax.ShapeDtypeStruct((groups, *pair_index.shape), pair_index.dtype),
         ),
-        in_specs=[VMEM_SPEC] * 3,
+        in_specs=[ANY_SPEC] * 3,
         out_specs=(ANY_SPEC,) * 3,
         scratch_shapes=[
-            dma((3,)), dma((groups,)), dma((groups,)), dma((groups,)), dma((groups,)),
+            pltpu.VMEM((rows, grid_points), orbitals.dtype),
+            dma((4,)), dma((groups,)), dma((groups,)), dma((groups,)), dma((groups,)),
             dma((2 * groups,)), dma((2 * groups,)),
             dma((groups,)), dma((groups,)), dma((groups,)), dma((groups,)),
+            dma((groups * slabs,)), dma((groups * slabs,)),
         ],
         compiler_params=pltpu.CompilerParams(collective_id=0, has_side_effects=True),
-    )(orbitals, trial_vectors, pair_index)
+    )(orbitals, parts, pair_index)
+    return table, trials.reshape(groups, batch, slots), pairs
 
 
 def density_kernel(pair_ref, trial_ref, table_ref, dens_ref, field_ref, turned):
@@ -229,22 +254,37 @@
 
 
 def apply_kernel(
-    count, slabs, field_ref, scale_ref, eig_ref, dens_ref, out_ref,
-    eig, dens, pieces, rs_in, slab_in, gathered, screened, potential, shares, share_in, slab_out,
-    load_sem, rs_send, rs_recv, sl_send, sl_recv, ag_send, ag_recv, d_send, d_recv, o_send, o_recv,
+    count, slabs, spans, field_ref, scale_ref, eig_ref, dens_ref, out_ref,
+    eig, dens, pieces, rs_in, slab_in, gathered, screened, potential, shares,
+    load_sem, rs_send, rs_recv, sl_send, sl_recv, ag_send, ag_recv, d_send, d_recv,
 ):
     me, slab = lax.axis_index("orb"), lax.axis_index("slab")
     groups = count // QUAD
     group, place = me // QUAD, lax.rem(me, QUAD)
     batch, width = field_ref.shape
-    slots = out_ref.shape[1]
+    slots = out_ref.shape[2]
+    members = count * spans
     tall = pieces.shape[1]
     bands = batch // tall
-    ranks = [lax.rem(me + k, count) for k in range(1, count)]
-    origins = [lax.rem(me + count - k, count) for k in range(1, count)]
+    mine = me * slabs + slab if spans > 1 else me
+    ranks = [lax.rem(mine + k, members) for k in range(1, members)]
+    origins = [lax.rem(mine + members - k, members) for k in range(1, members)]
     layers = [lax.rem(slab + k, slabs) for k in range(1, slabs)]
     layer_from = [lax.rem(slab + slabs - k, slabs) for k in range(1, slabs)]
-    ready = greet([{"orb": r} for r in ranks] + [{"slab": s} for s in layers])
+    goals = [lax.rem(group + k, groups) for k in range(1, groups)] + [group]
+
+    def member(rank):
+        if spans > 1:
+            return {"orb": rank // slabs, "slab": lax.rem(rank, slabs)}
+        return {"orb": rank, "slab": slab}
+
+    def keeper(g, x):
+        return {"orb": g * QUAD + place, "slab": x}
+
+    peers = [member(r) for r in ranks]
+    if spans == 1:
+        peers += [keeper(g, x) for g in goals for x in layers]
+    ready = greet(peers)
 
     load = pltpu.make_async_copy(eig_ref.at[:, columns(group, width)], eig, load_sem.at[0])
     load.start()
@@ -284,7 +324,7 @@
     def scatter(k, sender):
         return remote(
             pieces.at[ranks[k]], rs_in.at[sender], rs_send.at[k], rs_recv.at[sender],
-            {"orb": ranks[k]},
+            member(ranks[k]),
         )
 
     def layer_copy(k, sender):
@@ -296,30 +336,31 @@
     def gather(k, sender):
         return remote(
             gathered.at[sender], gathered.at[sender], ag_send.at[k], ag_recv.at[sender],
-            {"orb": ranks[k]},
+            member(ranks[k]),
         )
 
     ready()
-    for k in range(count - 1):
-        go(scatter(k, me))
-    total = pieces[me]
-    for k in range(count - 1):
+    for k in range(members - 1):
+        go(scatter(k, mine))
+    total = pieces[mine]
+    for k in range(members - 1):
         scatter(k, origins[k]).wait_recv()
         total = total + rs_in[origins[k]]
-    slab_in[slab] = total
-    for k in range(slabs - 1):
-        go(layer_copy(k, slab))
-    for k in range(slabs - 1):
-        layer_copy(k, layer_from[k]).wait_recv()
-    total = slab_in[0]
-    for s in range(1, slabs):
-        total = total + slab_in[s]
-    gathered[me] = total
-    for k in range(count - 1):
-        go(gather(k, me))
-    for k in range(count - 1):
+    if spans == 1:
+        slab_in[slab] = total
+        for k in range(slabs - 1):
+            go(layer_copy(k, slab))
+        for k in range(slabs - 1):
+            layer_copy(k, layer_from[k]).wait_recv()
+        total = slab_in[0]
+        for s in range(1, slabs):
+            total = total + slab_in[s]
+    gathered[mine] = total
+    for k in range(members - 1):
+        go(gather(k, mine))
+    for k in range(members - 1):
         gather(k, origins[k]).wait_recv()
-    for c in range(count // bands):
+    for c in range(members // bands):
         rows = jnp.concatenate([gathered[c * bands + h] for h in range(bands)], 0)
         cols = slice(c * LANES, (c + 1) * LANES)
         screened[:, cols] = split_rows(rows * scale_ref[:, cols])
@@ -339,40 +380,29 @@
             cols = columns(c, 256)
             shares[g, :, cols] = fold(
                 jnp.dot(potential[...], dens[g, :, cols], preferred_element_type=jnp.float32)
-            )
-
-    goals = [lax.rem(group + k, groups) for k in range(1, groups)]
-    givers = [lax.rem(group + groups - k, groups) for k in range(1, groups)]
-
-    def share_copy(k, sender):
-        return remote(
-            shares.at[goals[k]], share_in.at[sender], d_send.at[k], d_recv.at[sender],
-            {"orb": goals[k] * QUAD + place},
-        )
-
-    def out_copy(k, sender):
-        return remote(
-            slab_out.at[sender], slab_out.at[sender], o_send.at[k], o_recv.at[sender],
-            {"slab": layers[k]},
-        )
-
-    for k in range(groups - 1):
+            ).astype(shares.dtype)
+
+    givers = [lax.rem(group + groups - k, groups) for k in range(1, groups)] + [group]
+
+    def share_copy(k, n, g, x):
+        slot = k * slabs + n
+        return remote(
+            shares.at[goals[k]], out_ref.at[g * slabs + x], d_send.at[slot], d_recv.at[slot],
+            keeper(goals[k], layers[n] if n < slabs - 1 else slab),
+        )
+
+    for k in range(groups):
         apply_to(goals[k])
-        go(share_copy(k, group))
-    apply_to(group)
-    total = shares[group]
-    for k in range(groups - 1):
-        share_copy(k, givers[k]).wait_recv()
-        total = total + share_in[givers[k]]
-    slab_out[slab] = total
-    for k in range(slabs - 1):
-        go(out_copy(k, slab))
-    for k in range(slabs - 1):
-        out_copy(k, layer_from[k]).wait_recv()
-    total = slab_out[0]
-    for s in range(1, slabs):
-        total = total + slab_out[s]
-    out_ref[...] = total
+        for n in range(slabs if k < groups - 1 else slabs - 1):
+            go(share_copy(k, n, group, slab))
+    own = pltpu.make_async_copy(
+        shares.at[group], out_ref.at[group * slabs + slab], load_sem.at[0]
+    )
+    own.start()
+    for k in range(groups):
+        for n in range(slabs if k < groups - 1 else slabs - 1):
+            share_copy(k, n, givers[k], layer_from[n] if n < slabs - 1 else slab).wait_recv()
+    own.wait()
     for copy in sent:
         copy.wait_send()
 
@@ -381,37 +411,38 @@
     groups = count // QUAD
     batch, width = field.shape
     neig = eigenpotentials.shape[0]
-    tall = batch * neig // (count * LANES)
+    spans = slabs if batch * neig % (count * slabs * LANES) == 0 else 1
+    members = count * spans
+    tall = batch * neig // (members * LANES)
     dma = pltpu.SemaphoreType.DMA
     f32, b16 = jnp.float32, jnp.bfloat16
-    return pl.pallas_call(
-        functools.partial(apply_kernel, count, slabs),
-        out_shape=jax.ShapeDtypeStruct((batch, slots), f32),
+    parts = pl.pallas_call(
+        functools.partial(apply_kernel, count, slabs, spans),
+        out_shape=jax.ShapeDtypeStruct((groups * slabs, batch, slots), b16),
         in_specs=[VMEM_SPEC, VMEM_SPEC, ANY_SPEC, ANY_SPEC],
-        out_specs=VMEM_SPEC,
+        out_specs=ANY_SPEC,
         scratch_shapes=[
             pltpu.VMEM((neig, width), b16),
             pltpu.VMEM((groups, width, slots), b16),
-            pltpu.VMEM((count, tall, LANES), f32),
-            pltpu.VMEM((count, tall, LANES), f32),
+            pltpu.VMEM((members, tall, LANES), f32),
+            pltpu.VMEM((members, tall, LANES), f32),
             pltpu.VMEM((slabs, tall, LANES), f32),
-            pltpu.VMEM((count, tall, LANES), f32),
+            pltpu.VMEM((members, tall, LANES), f32),
             pltpu.VMEM((2 * batch, neig), b16),
             pltpu.VMEM((2 * batch, width), b16),
-            pltpu.VMEM((groups, batch, slots), f32),
-            pltpu.VMEM((groups, batch, slots), f32),
-            pltpu.VMEM((slabs, batch, slots), f32),
+            pltpu.VMEM((groups, batch, slots), b16),
             dma((1 + groups,)),
-            dma((count,)), dma((count,)), dma((slabs,)), dma((slabs,)),
-            dma((count,)), dma((count,)), dma((groups,)), dma((groups,)),
-            dma((slabs,)), dma((slabs,)),
+            dma((members,)), dma((members,)), dma((slabs,)), dma((slabs,)),
+            dma((members,)), dma((members,)),
+            dma((groups * slabs,)), dma((groups * slabs,)),
         ],
         compiler_params=pltpu.CompilerParams(collective_id=1, has_side_effects=True),
     )(field, screening.reshape(1, neig), eigenpotentials, dens)
+    return jnp.sum(parts.astype(f32), 0)
 
 
 def shards(count, slabs, orbitals, eigenpotentials, screening, trial_vectors, pair_index):
-    table, trials, pairs = spread(count, orbitals, trial_vectors, pair_index)
+    table, trials, pairs = spread(count, slabs, orbitals, trial_vectors, pair_index)
     dens, field = densities(pairs, trials, table)
     slots = trial_vectors.shape[1]
     return apply_direct(count, slabs, field, screening, eigenpotentials, dens, slots)

time: 65.4 us -> 61.6 us (0.942)
  Pallas kernels: 63.7 us -> 59.7 us
  other arithmetic: 0 us -> 1.62 us
  local copies, waits for them, and re-layouts: 1.47 us -> 0 us
    pallas_call x2, Pallas kernels: 49.8 us -> 45.1 us  [the longest x1 24.9 us: apply_direct(): pl.pallas_call(functools.partial(apply_kernel, count, slabs, spans), out_...]
    reduce_sum x0 -> x1, other arithmetic: none -> 1.62 us  [apply_direct(): return jnp.sum(parts.astype(f32), 0)]
    unnamed x1 -> x0, local copies, waits for them, and re-layouts: 1.47 us -> none
    pallas_call x1, Pallas kernels: 13.9 us -> 14.6 us  [densities(): pl.pallas_call(density_kernel, grid=(groups, steps), out_shape=(jax.Shape...]
where the time goes in v2:
time: 61.6 us; the launch traced here: 61.4 us
  Pallas kernels  59.7 us (97%)
  other arithmetic  1.62 us (3%)
    pallas_call x1, Pallas kernels, apply_direct(): pl.pallas_call(functools.partial(apply_kernel, count, slabs, spans), out_...  24.9 us
    pallas_call x1, Pallas kernels, spread(): pl.pallas_call(functools.partial(spread_kernel, groups, slabs), out_shape...  20.2 us
    pallas_call x1, Pallas kernels, densities(): pl.pallas_call(density_kernel, grid=(groups, steps), out_shape=(jax.Shape...  14.6 us
    reduce_sum x1, other arithmetic, apply_direct(): return jnp.sum(parts.astype(f32), 0)  1.62 us

profile of v2, /device:TPU:0, one launch (start us, length us, event | category | flops | bytes accessed | tf_op | source)
XLA Modules:
  0.0 61.4 jit_solution(14277306610832450825)
XLA Ops:
  0.0 20.2 %shard_map.55 = (bf16[16,32,1024]{2,1,0:T(8,128)(2,1)}, bf16[4,2,8,1024]{3,2,1,0:T(8,128)(2,1)}, s32[4,2,1024]{2,1,0:T(2,128)}) custom-call(bf16[32,4096]{1,0:T(8,128)(2,1)} %orb_hbm.1, bf16[2,8,1024]{2,1,0:T(8,128)(2,1)} %bitcast.6, s32[2,1024]{1,0:T(2,128)} %pair_ref.1), custom_call_target="tpu_custom_call" | custom-call | tf_op jit(solution)/shard_map/pallas_call | solution.py:160
  20.3 14.6 %shard_map.56 = (bf16[1024,4096]{1,0:T(8,128)(2,1)}, f32[16,1024]{1,0:T(8,128)}) custom-call(s32[4,2,1024]{2,1,0:T(2,128)} %get-tuple-element.10.pair_ref, bf16[4,16,1024]{2,1,0:T(8,128)(2,1)} %bitcast.5, bf16[512,1024]{1,0:T(8,128)(2,1)} %bitcast.4), custom_call_target="tpu_custom_call" | custom-call | tf_op jit(solution)/shard_map/pallas_call | solution.py:225
  34.8 24.9 %shard_map.57 = bf16[8,16,1024]{2,1,0:T(8,128)(2,1)} custom-call(f32[16,1024]{1,0:T(8,128)} %get-tuple-element.13.field_ref, f32[1,1024]{1,0:T(1,128)} %bitcast.7, bf16[1024,4096]{1,0:T(8,128)(2,1)} %eig_ref.1, bf16[1024,4096]{1,0:T(8,128)(2,1)} %get-tuple-element.14.dens_ref), custom_call_target="tpu_custom_call" | custom-call | tf_op jit(solution)/shard_map/pallas_call | solution.py:419
  59.7 1.6 %convert_reduce_fusion = f32[16,1024]{1,0:T(8,128)} fusion(bf16[8,16,1024]{2,1,0:T(8,128)(2,1)} %shard_map.57), kind=kLoop, calls=%fused_computation | loop fusion | flops 245760 | bytes 327680 | tf_op jit(solution)/shard_map/reduce_sum | solution.py:441

commit v3 on v2

--- a/solution.py
+++ b/solution.py
@@ -19,6 +19,15 @@
     for peer in peers:
         pl.semaphore_signal(barrier, inc=1, device_id=peer, device_id_type=MESH_ID)
     return lambda: pl.semaphore_wait(barrier, len(peers))
+
+
+def flip(index, mask, extent):
+    total, bit = 0, 1
+    while bit < extent:
+        digit = lax.rem(index // bit, 2)
+        total = total + bit * (1 - digit if mask & bit else digit)
+        bit *= 2
+    return total
 
 
 def columns(start, size):
@@ -41,8 +50,8 @@
     def device(g, q):
         return {"orb": g * QUAD + q}
 
-    others = [lax.rem(group + k, groups) for k in range(1, groups)]
-    sources = [lax.rem(group + groups - k, groups) for k in range(1, groups)]
+    others = [flip(group, k, groups) for k in range(groups - 1, 0, -1)]
+    sources = others
     layers = [lax.rem(slab + k, slabs) for k in range(1, slabs)]
     layer_from = [lax.rem(slab + slabs - k, slabs) for k in range(1, slabs)]
     ready = greet(
@@ -254,36 +263,34 @@
 
 
 def apply_kernel(
-    count, slabs, spans, field_ref, scale_ref, eig_ref, dens_ref, out_ref,
-    eig, dens, pieces, rs_in, slab_in, gathered, screened, potential, shares,
-    load_sem, rs_send, rs_recv, sl_send, sl_recv, ag_send, ag_recv, d_send, d_recv,
+    count, slabs, field_ref, scale_ref, eig_ref, dens_ref, out_ref,
+    eig, dens, pieces, rs_in, outer_in, gathered, screened, potential, shares,
+    load_sem, rs_send, rs_recv, z_send, z_recv, ag_send, ag_recv, d_send, d_recv,
 ):
     me, slab = lax.axis_index("orb"), lax.axis_index("slab")
     groups = count // QUAD
     group, place = me // QUAD, lax.rem(me, QUAD)
     batch, width = field_ref.shape
     slots = out_ref.shape[2]
-    members = count * spans
+    members = QUAD * slabs
     tall = pieces.shape[1]
     bands = batch // tall
-    mine = me * slabs + slab if spans > 1 else me
+    mine = place * slabs + slab
     ranks = [lax.rem(mine + k, members) for k in range(1, members)]
     origins = [lax.rem(mine + members - k, members) for k in range(1, members)]
     layers = [lax.rem(slab + k, slabs) for k in range(1, slabs)]
     layer_from = [lax.rem(slab + slabs - k, slabs) for k in range(1, slabs)]
-    goals = [lax.rem(group + k, groups) for k in range(1, groups)] + [group]
+    outers = [flip(group, k, groups) for k in range(groups - 1, 0, -1)]
+    goals = outers + [group]
 
     def member(rank):
-        if spans > 1:
-            return {"orb": rank // slabs, "slab": lax.rem(rank, slabs)}
-        return {"orb": rank, "slab": slab}
+        return {"orb": group * QUAD + rank // slabs, "slab": lax.rem(rank, slabs)}
 
     def keeper(g, x):
         return {"orb": g * QUAD + place, "slab": x}
 
     peers = [member(r) for r in ranks]
-    if spans == 1:
-        peers += [keeper(g, x) for g in goals for x in layers]
+    peers += [keeper(g, x) for g in outers for x in layers + [slab]]
     ready = greet(peers)
 
     load = pltpu.make_async_copy(eig_ref.at[:, columns(group, width)], eig, load_sem.at[0])
@@ -327,10 +334,10 @@
             member(ranks[k]),
         )
 
-    def layer_copy(k, sender):
-        return remote(
-            slab_in.at[sender], slab_in.at[sender], sl_send.at[k], sl_recv.at[sender],
-            {"slab": layers[k]},
+    def outer_copy(k, sender):
+        return remote(
+            outer_in.at[sender], outer_in.at[sender], z_send.at[k], z_recv.at[k],
+            keeper(outers[k], slab),
         )
 
     def gather(k, sender):
@@ -346,15 +353,14 @@
     for k in range(members - 1):
         scatter(k, origins[k]).wait_recv()
         total = total + rs_in[origins[k]]
-    if spans == 1:
-        slab_in[slab] = total
-        for k in range(slabs - 1):
-            go(layer_copy(k, slab))
-        for k in range(slabs - 1):
-            layer_copy(k, layer_from[k]).wait_recv()
-        total = slab_in[0]
-        for s in range(1, slabs):
-            total = total + slab_in[s]
+    outer_in[group] = total
+    for k in range(groups - 1):
+        go(outer_copy(k, group))
+    for k in range(groups - 1):
+        outer_copy(k, outers[k]).wait_recv()
+    total = outer_in[0]
+    for g in range(1, groups):
+        total = total + outer_in[g]
     gathered[mine] = total
     for k in range(members - 1):
         go(gather(k, mine))
@@ -381,8 +387,6 @@
             shares[g, :, cols] = fold(
                 jnp.dot(potential[...], dens[g, :, cols], preferred_element_type=jnp.float32)
             ).astype(shares.dtype)
-
-    givers = [lax.rem(group + groups - k, groups) for k in range(1, groups)] + [group]
 
     def share_copy(k, n, g, x):
         slot = k * slabs + n
@@ -401,7 +405,7 @@
     own.start()
     for k in range(groups):
         for n in range(slabs if k < groups - 1 else slabs - 1):
-            share_copy(k, n, givers[k], layer_from[n] if n < slabs - 1 else slab).wait_recv()
+            share_copy(k, n, goals[k], layer_from[n] if n < slabs - 1 else slab).wait_recv()
     own.wait()
     for copy in sent:
         copy.wait_send()
@@ -411,13 +415,12 @@
     groups = count // QUAD
     batch, width = field.shape
     neig = eigenpotentials.shape[0]
-    spans = slabs if batch * neig % (count * slabs * LANES) == 0 else 1
-    members = count * spans
+    members = QUAD * slabs
     tall = batch * neig // (members * LANES)
     dma = pltpu.SemaphoreType.DMA
     f32, b16 = jnp.float32, jnp.bfloat16
     parts = pl.pallas_call(
-        functools.partial(apply_kernel, count, slabs, spans),
+        functools.partial(apply_kernel, count, slabs),
         out_shape=jax.ShapeDtypeStruct((groups * slabs, batch, slots), b16),
         in_specs=[VMEM_SPEC, VMEM_SPEC, ANY_SPEC, ANY_SPEC],
         out_specs=ANY_SPEC,
@@ -426,13 +429,13 @@
             pltpu.VMEM((groups, width, slots), b16),
             pltpu.VMEM((members, tall, LANES), f32),
             pltpu.VMEM((members, tall, LANES), f32),
-            pltpu.VMEM((slabs, tall, LANES), f32),
+            pltpu.VMEM((groups, tall, LANES), f32),
             pltpu.VMEM((members, tall, LANES), f32),
             pltpu.VMEM((2 * batch, neig), b16),
             pltpu.VMEM((2 * batch, width), b16),
             pltpu.VMEM((groups, batch, slots), b16),
             dma((1 + groups,)),
-            dma((members,)), dma((members,)), dma((slabs,)), dma((slabs,)),
+            dma((members,)), dma((members,)), dma((groups,)), dma((groups,)),
             dma((members,)), dma((members,)),
             dma((groups * slabs,)), dma((groups * slabs,)),
         ],

time: 61.6 us -> 61.8 us (level); the launches traced: 61.4 us -> 60.8 us
    pallas_call x1, Pallas kernels: 20.2 us -> 21.9 us  [spread(): pl.pallas_call(functools.partial(spread_kernel, groups, slabs), out_shape...]
    pallas_call x1, Pallas kernels: 24.9 us -> 23.5 us  [apply_direct(): pl.pallas_call(functools.partial(apply_kernel, count, slabs), out_shape=j...]
    pallas_call x1, Pallas kernels: 14.6 us -> 13.8 us  [densities(): pl.pallas_call(density_kernel, grid=(groups, steps), out_shape=(jax.Shape...]
where the time goes in v3:
time: 61.8 us; the launch traced here: 60.8 us
  Pallas kernels  59.2 us (96%)
  other arithmetic  1.62 us (3%)
    pallas_call x1, Pallas kernels, apply_direct(): pl.pallas_call(functools.partial(apply_kernel, count, slabs), out_shape=j...  23.5 us
    pallas_call x1, Pallas kernels, spread(): pl.pallas_call(functools.partial(spread_kernel, groups, slabs), out_shape...  21.9 us
    pallas_call x1, Pallas kernels, densities(): pl.pallas_call(density_kernel, grid=(groups, steps), out_shape=(jax.Shape...  13.8 us
    reduce_sum x1, other arithmetic, apply_direct(): return jnp.sum(parts.astype(f32), 0)  1.62 us

profile of v3, /device:TPU:0, one launch (start us, length us, event | category | flops | bytes accessed | tf_op | source)
XLA Modules:
  0.0 60.8 jit_solution(14647239306278683497)
XLA Ops:
  0.0 21.9 %shard_map.55 = (bf16[16,32,1024]{2,1,0:T(8,128)(2,1)}, bf16[4,2,8,1024]{3,2,1,0:T(8,128)(2,1)}, s32[4,2,1024]{2,1,0:T(2,128)}) custom-call(bf16[32,4096]{1,0:T(8,128)(2,1)} %orb_hbm.1, bf16[2,8,1024]{2,1,0:T(8,128)(2,1)} %bitcast.6, s32[2,1024]{1,0:T(2,128)} %pair_ref.1), custom_call_target="tpu_custom_call" | custom-call | tf_op jit(solution)/shard_map/pallas_call | solution.py:169
  22.0 13.8 %shard_map.56 = (bf16[1024,4096]{1,0:T(8,128)(2,1)}, f32[16,1024]{1,0:T(8,128)}) custom-call(s32[4,2,1024]{2,1,0:T(2,128)} %get-tuple-element.10.pair_ref, bf16[4,16,1024]{2,1,0:T(8,128)(2,1)} %bitcast.5, bf16[512,1024]{1,0:T(8,128)(2,1)} %bitcast.4), custom_call_target="tpu_custom_call" | custom-call | tf_op jit(solution)/shard_map/pallas_call | solution.py:234
  35.7 23.5 %shard_map.57 = bf16[8,16,1024]{2,1,0:T(8,128)(2,1)} custom-call(f32[16,1024]{1,0:T(8,128)} %get-tuple-element.13.field_ref, f32[1,1024]{1,0:T(1,128)} %bitcast.7, bf16[1024,4096]{1,0:T(8,128)(2,1)} %eig_ref.1, bf16[1024,4096]{1,0:T(8,128)(2,1)} %get-tuple-element.14.dens_ref), custom_call_target="tpu_custom_call" | custom-call | tf_op jit(solution)/shard_map/pallas_call | solution.py:422
  59.2 1.6 %convert_reduce_fusion = f32[16,1024]{1,0:T(8,128)} fusion(bf16[8,16,1024]{2,1,0:T(8,128)(2,1)} %shard_map.57), kind=kLoop, calls=%fused_computation | loop fusion | flops 245760 | bytes 327680 | tf_op jit(solution)/shard_map/reduce_sum | solution.py:444

commit v4 on v3

--- a/solution.py
+++ b/solution.py
@@ -50,8 +50,8 @@
     def device(g, q):
         return {"orb": g * QUAD + q}
 
-    others = [flip(group, k, groups) for k in range(groups - 1, 0, -1)]
-    sources = others
+    others = [lax.rem(group + k, groups) for k in range(1, groups)]
+    sources = [lax.rem(group + groups - k, groups) for k in range(1, groups)]
     layers = [lax.rem(slab + k, slabs) for k in range(1, slabs)]
     layer_from = [lax.rem(slab + slabs - k, slabs) for k in range(1, slabs)]
     ready = greet(
@@ -187,42 +187,50 @@
     return table, trials.reshape(groups, batch, slots), pairs
 
 
-def density_kernel(pair_ref, trial_ref, table_ref, dens_ref, field_ref, turned):
-    first_step = (pl.program_id(0) == 0) & (pl.program_id(1) == 0)
-
-    @pl.when(first_step)
-    def _():
-        turned[...] = table_ref[...].T
-        field_ref[...] = jnp.zeros_like(field_ref)
-
-    index = pair_ref[0]
-    is_live = jnp.max(index) >= 0
-
-    @pl.when(is_live)
-    def _():
-        orbs = turned.shape[1]
-        ids = lax.broadcasted_iota(jnp.int32, (orbs, index.shape[1]), 0)
-
-        def pick(row):
-            return jnp.where(ids == index[row : row + 1], 1.0, 0.0).astype(jnp.bfloat16)
-
-        left, right = pick(0), pick(1)
-        trial = trial_ref[0]
-        step = min(512, turned.shape[0])
-        for c in range(turned.shape[0] // step):
-            rows = pl.ds(c * step, step)
-            part = turned[rows, :]
-            one = jnp.dot(part, left, preferred_element_type=jnp.float32)
-            two = jnp.dot(part, right, preferred_element_type=jnp.float32)
-            dens = (one * two).astype(jnp.bfloat16)
-            dens_ref[rows, :] = dens
-            field_ref[:, rows] += lax.dot_general(
-                trial, dens, (((1,), (1,)), ((), ())), preferred_element_type=jnp.float32
-            )
-
-    @pl.when(jnp.logical_not(is_live))
-    def _():
-        dens_ref[...] = jnp.zeros_like(dens_ref)
+def density_kernel(pair_ref, trial_ref, table_ref, dens_ref, field_ref, turned, blocks, sems):
+    count, width, block = blocks.shape
+    steps = trial_ref.shape[2] // block
+    orbs = turned.shape[1]
+    turned[...] = table_ref[...].T
+    field_ref[...] = jnp.zeros_like(field_ref)
+
+    def block_index(b):
+        return pair_ref[b // steps, :, columns(lax.rem(b, steps), block)]
+
+    def write_out(b):
+        return pltpu.make_async_copy(blocks.at[b], dens_ref.at[:, columns(b, block)], sems.at[b])
+
+    @pl.loop(0, count)
+    def _(b):
+        index = block_index(b)
+
+        @pl.when(jnp.max(index) >= 0)
+        def _():
+            ids = lax.broadcasted_iota(jnp.int32, (orbs, block), 0)
+
+            def pick(row):
+                return jnp.where(ids == index[row : row + 1], 1.0, 0.0).astype(jnp.bfloat16)
+
+            left, right = pick(0), pick(1)
+            trial = trial_ref[b // steps, :, columns(lax.rem(b, steps), block)]
+            step = min(512, width)
+            for c in range(width // step):
+                rows = pl.ds(c * step, step)
+                part = turned[rows, :]
+                one = jnp.dot(part, left, preferred_element_type=jnp.float32)
+                two = jnp.dot(part, right, preferred_element_type=jnp.float32)
+                dens = (one * two).astype(jnp.bfloat16)
+                blocks[b, rows, :] = dens
+                field_ref[:, rows] += lax.dot_general(
+                    trial, dens, (((1,), (1,)), ((), ())), preferred_element_type=jnp.float32
+                )
+            write_out(b).start()
+
+    @pl.loop(0, count)
+    def _(b):
+        @pl.when(jnp.max(block_index(b)) >= 0)
+        def _():
+            write_out(b).wait()
 
 
 def densities(pairs, trials, table):
@@ -230,24 +238,20 @@
     count, rows, width = table.shape
     orbs = count * rows
     block = min(512, slots)
-    steps = slots // block
+    blocks = groups * slots // block
     return pl.pallas_call(
         density_kernel,
-        grid=(groups, steps),
         out_shape=(
             jax.ShapeDtypeStruct((width, groups * slots), jnp.bfloat16),
             jax.ShapeDtypeStruct((batch, width), jnp.float32),
         ),
-        in_specs=[
-            pl.BlockSpec((1, 2, block), lambda g, i: (g, 0, i)),
-            pl.BlockSpec((1, batch, block), lambda g, i: (g, 0, i)),
-            pl.BlockSpec((orbs, width), lambda g, i: (0, 0)),
+        in_specs=[VMEM_SPEC] * 3,
+        out_specs=(ANY_SPEC, VMEM_SPEC),
+        scratch_shapes=[
+            pltpu.VMEM((width, orbs), jnp.bfloat16),
+            pltpu.VMEM((blocks, width, block), jnp.bfloat16),
+            pltpu.SemaphoreType.DMA((blocks,)),
         ],
-        out_specs=(
-            pl.BlockSpec((width, block), lambda g, i: (0, g * steps + i)),
-            pl.BlockSpec((batch, width), lambda g, i: (0, 0)),
-        ),
-        scratch_shapes=[pltpu.VMEM((width, orbs), jnp.bfloat16)],
     )(pairs, trials, table.reshape(orbs, width))
 
 
@@ -448,7 +452,8 @@
     table, trials, pairs = spread(count, slabs, orbitals, trial_vectors, pair_index)
     dens, field = densities(pairs, trials, table)
     slots = trial_vectors.shape[1]
-    return apply_direct(count, slabs, field, screening, eigenpotentials, dens, slots)
+    direct = apply_direct(count, slabs, field, screening, eigenpotentials, dens, slots)
+    return jnp.where(pair_index[:1] >= 0, direct, 0.0)
 
 
 def solution(mesh):

time: 61.8 us -> 61.2 us (level); the launches traced: 60.8 us -> 61.3 us
    pallas_call x1, Pallas kernels: 21.9 us -> 20.2 us  [spread(): pl.pallas_call(functools.partial(spread_kernel, groups, slabs), out_shape...]
    pallas_call x1, Pallas kernels: 23.5 us -> 25.1 us  [apply_direct(): pl.pallas_call(functools.partial(apply_kernel, count, slabs), out_shape=j...]
    select_n x0 -> x1, other arithmetic: none -> 0.64 us  [shards(): return jnp.where(pair_index[:1] >= 0, direct, 0.0)]
    reduce_sum x1, other arithmetic: 1.62 us -> 1 us  [apply_direct(): return jnp.sum(parts.astype(f32), 0)]
where the time goes in v4:
time: 61.2 us; the launch traced here: 61.3 us
  Pallas kernels  59.6 us (97%)
  other arithmetic  1.66 us (3%)
    pallas_call x1, Pallas kernels, apply_direct(): pl.pallas_call(functools.partial(apply_kernel, count, slabs), out_shape=j...  25.1 us
    pallas_call x1, Pallas kernels, spread(): pl.pallas_call(functools.partial(spread_kernel, groups, slabs), out_shape...  20.2 us
    pallas_call x1, Pallas kernels, densities(): pl.pallas_call(density_kernel, out_shape=(jax.ShapeDtypeStruct((width, gr...  14.2 us

profile of v4, /device:TPU:0, one launch (start us, length us, event | category | flops | bytes accessed | tf_op | source)
XLA Modules:
  0.0 61.3 jit_solution(16047375797833998622)
XLA Ops:
  0.0 20.2 %shard_map.55 = (bf16[16,32,1024]{2,1,0:T(8,128)(2,1)}, bf16[4,2,8,1024]{3,2,1,0:T(8,128)(2,1)}, s32[4,2,1024]{2,1,0:T(2,128)}) custom-call(bf16[32,4096]{1,0:T(8,128)(2,1)} %orb_hbm.1, bf16[2,8,1024]{2,1,0:T(8,128)(2,1)} %bitcast.6, s32[2,1024]{1,0:T(2,128)} %pair_ref.1), custom_call_target="tpu_custom_call" | custom-call | tf_op jit(solution)/shard_map/pallas_call | solution.py:169
  20.3 14.2 %shard_map.56 = (bf16[1024,4096]{1,0:T(8,128)(2,1)}, f32[16,1024]{1,0:T(8,128)}) custom-call(s32[4,2,1024]{2,1,0:T(2,128)} %get-tuple-element.10.pair_ref, bf16[4,16,1024]{2,1,0:T(8,128)(2,1)} %bitcast.5, bf16[512,1024]{1,0:T(8,128)(2,1)} %bitcast.4), custom_call_target="tpu_custom_call" | custom-call | tf_op jit(solution)/shard_map/pallas_call | solution.py:242
  34.5 0.0 copy-start
  34.5 25.1 %shard_map.57 = bf16[8,16,1024]{2,1,0:T(8,128)(2,1)} custom-call(f32[16,1024]{1,0:T(8,128)} %get-tuple-element.13.field_ref, f32[1,1024]{1,0:T(1,128)} %bitcast.7, bf16[1024,4096]{1,0:T(8,128)(2,1)} %eig_ref.1, bf16[1024,4096]{1,0:T(8,128)(2,1)} %get-tuple-element.14.dens_ref), custom_call_target="tpu_custom_call" | custom-call | tf_op jit(solution)/shard_map/pallas_call | solution.py:426
  59.6 1.0 %convert_reduce_fusion = f32[16,1024]{1,0:T(8,128)S(1)} fusion(bf16[8,16,1024]{2,1,0:T(8,128)(2,1)} %shard_map.57), kind=kLoop, calls=%fused_computation | loop fusion | flops 245760 | bytes 327680 | tf_op jit(solution)/shard_map/reduce_sum | solution.py:448
  60.6 0.0 copy-done
  60.7 0.6 %broadcast_select_fusion = f32[16,1024]{1,0:T(8,128)} fusion(f32[16,1024]{1,0:T(8,128)S(1)} %convert_reduce_fusion, pred[1024]{0:T(1024)(128)(4,1)S(1)} %compare_reduce_fusion), kind=kLoop, calls=%fused_computation.1 | loop fusion | flops 16384 | bytes 132096 | tf_op jit(solution)/shard_map/jit(_where)/select_n | solution.py:456
  (1 shorter events, 0.0 us)
Async XLA Ops:
  34.5 26.2 %copy-start = (s32[2,1024]{1,0:T(2,128)S(1)}, s32[2,1024]{1,0:T(2,128)}, u32[]{:S(2)}) copy-start(s32[2,1024]{1,0:T(2,128)} %pair_ref.1) | copy-start | bytes 24580

commit v5 on v4

--- a/solution.py
+++ b/solution.py
@@ -187,18 +187,17 @@
     return table, trials.reshape(groups, batch, slots), pairs
 
 
-def density_kernel(pair_ref, trial_ref, table_ref, dens_ref, field_ref, turned, blocks, sems):
-    count, width, block = blocks.shape
+def density_kernel(pair_ref, trial_ref, table_ref, dens_ref, field_ref, blocks, sems):
+    count, block, width = blocks.shape
     steps = trial_ref.shape[2] // block
-    orbs = turned.shape[1]
-    turned[...] = table_ref[...].T
+    orbs = table_ref.shape[0]
     field_ref[...] = jnp.zeros_like(field_ref)
 
     def block_index(b):
         return pair_ref[b // steps, :, columns(lax.rem(b, steps), block)]
 
     def write_out(b):
-        return pltpu.make_async_copy(blocks.at[b], dens_ref.at[:, columns(b, block)], sems.at[b])
+        return pltpu.make_async_copy(blocks.at[b], dens_ref.at[columns(b, block)], sems.at[b])
 
     @pl.loop(0, count)
     def _(b):
@@ -206,24 +205,24 @@
 
         @pl.when(jnp.max(index) >= 0)
         def _():
-            ids = lax.broadcasted_iota(jnp.int32, (orbs, block), 0)
+            ids = lax.broadcasted_iota(jnp.int32, (block, orbs), 1)
+            upright = jnp.concatenate([index] * 4, 0).T
 
             def pick(row):
-                return jnp.where(ids == index[row : row + 1], 1.0, 0.0).astype(jnp.bfloat16)
+                hits = ids == upright[:, row : row + 1]
+                return jnp.where(hits, 1.0, 0.0).astype(jnp.bfloat16)
 
             left, right = pick(0), pick(1)
             trial = trial_ref[b // steps, :, columns(lax.rem(b, steps), block)]
             step = min(512, width)
             for c in range(width // step):
-                rows = pl.ds(c * step, step)
-                part = turned[rows, :]
-                one = jnp.dot(part, left, preferred_element_type=jnp.float32)
-                two = jnp.dot(part, right, preferred_element_type=jnp.float32)
+                cols = pl.ds(c * step, step)
+                part = table_ref[:, cols]
+                one = jnp.dot(left, part, preferred_element_type=jnp.float32)
+                two = jnp.dot(right, part, preferred_element_type=jnp.float32)
                 dens = (one * two).astype(jnp.bfloat16)
-                blocks[b, rows, :] = dens
-                field_ref[:, rows] += lax.dot_general(
-                    trial, dens, (((1,), (1,)), ((), ())), preferred_element_type=jnp.float32
-                )
+                blocks[b, :, cols] = dens
+                field_ref[:, cols] += jnp.dot(trial, dens, preferred_element_type=jnp.float32)
             write_out(b).start()
 
     @pl.loop(0, count)
@@ -242,14 +241,13 @@
     return pl.pallas_call(
         density_kernel,
         out_shape=(
-            jax.ShapeDtypeStruct((width, groups * slots), jnp.bfloat16),
+            jax.ShapeDtypeStruct((groups * slots, width), jnp.bfloat16),
             jax.ShapeDtypeStruct((batch, width), jnp.float32),
         ),
         in_specs=[VMEM_SPEC] * 3,
         out_specs=(ANY_SPEC, VMEM_SPEC),
         scratch_shapes=[
-            pltpu.VMEM((width, orbs), jnp.bfloat16),
-            pltpu.VMEM((blocks, width, block), jnp.bfloat16),
+            pltpu.VMEM((blocks, block, width), jnp.bfloat16),
             pltpu.SemaphoreType.DMA((blocks,)),
         ],
     )(pairs, trials, table.reshape(orbs, width))
@@ -301,7 +299,7 @@
     load.start()
     dens_loads = [
         pltpu.make_async_copy(
-            dens_ref.at[:, pl.ds(g * slots, slots)], dens.at[g], load_sem.at[1 + g]
+            dens_ref.at[pl.ds(g * slots, slots)], dens.at[g], load_sem.at[1 + g]
         )
         for g in range(groups)
     ]
@@ -389,7 +387,10 @@
         def _(c):
             cols = columns(c, 256)
             shares[g, :, cols] = fold(
-                jnp.dot(potential[...], dens[g, :, cols], preferred_element_type=jnp.float32)
+                lax.dot_general(
+                    potential[...], dens[g, cols, :], (((1,), (1,)), ((), ())),
+                    preferred_element_type=jnp.float32,
+                )
             ).astype(shares.dtype)
 
     def share_copy(k, n, g, x):
@@ -430,7 +431,7 @@
         out_specs=ANY_SPEC,
         scratch_shapes=[
             pltpu.VMEM((neig, width), b16),
-            pltpu.VMEM((groups, width, slots), b16),
+            pltpu.VMEM((groups, slots, width), b16),
             pltpu.VMEM((members, tall, LANES), f32),
             pltpu.VMEM((members, tall, LANES), f32),
             pltpu.VMEM((groups, tall, LANES), f32),
@@ -445,15 +446,16 @@
         ],
         compiler_params=pltpu.CompilerParams(collective_id=1, has_side_effects=True),
     )(field, screening.reshape(1, neig), eigenpotentials, dens)
-    return jnp.sum(parts.astype(f32), 0)
+    return parts
 
 
 def shards(count, slabs, orbitals, eigenpotentials, screening, trial_vectors, pair_index):
     table, trials, pairs = spread(count, slabs, orbitals, trial_vectors, pair_index)
     dens, field = densities(pairs, trials, table)
     slots = trial_vectors.shape[1]
-    direct = apply_direct(count, slabs, field, screening, eigenpotentials, dens, slots)
-    return jnp.where(pair_index[:1] >= 0, direct, 0.0)
+    parts = apply_direct(count, slabs, field, screening, eigenpotentials, dens, slots)
+    is_live = pair_index[:1][None] >= 0
+    return jnp.sum(jnp.where(is_live, parts.astype(jnp.float32), 0.0), 0)
 
 
 def solution(mesh):

time: 61.2 us -> 60.4 us (0.987)
  Pallas kernels: 59.6 us -> 58.5 us
    pallas_call x1, Pallas kernels: 14.2 us -> 12.8 us  [densities(): pl.pallas_call(density_kernel, out_shape=(jax.ShapeDtypeStruct((groups *...]
    reduce_sum x1, other arithmetic: 1 us -> 1.64 us  [shards(): return jnp.sum(jnp.where(is_live, parts.astype(jnp.float32), 0.0), 0)]
    select_n x1 -> x0, other arithmetic: 0.64 us -> none  [shards(): return jnp.where(pair_index[:1] >= 0, direct, 0.0)]
where the time goes in v5:
time: 60.4 us; the launch traced here: 60.2 us
  Pallas kernels  58.5 us (97%)
  other arithmetic  1.67 us (3%)
    pallas_call x1, Pallas kernels, apply_direct(): pl.pallas_call(functools.partial(apply_kernel, count, slabs), out_shape=j...  25.4 us
    pallas_call x1, Pallas kernels, spread(): pl.pallas_call(functools.partial(spread_kernel, groups, slabs), out_shape...  20.2 us
    pallas_call x1, Pallas kernels, densities(): pl.pallas_call(density_kernel, out_shape=(jax.ShapeDtypeStruct((groups *...  12.8 us
    reduce_sum x1, other arithmetic, shards(): return jnp.sum(jnp.where(is_live, parts.astype(jnp.float32), 0.0), 0)  1.64 us

profile of v5, /device:TPU:0, one launch (start us, length us, event | category | flops | bytes accessed | tf_op | source)
XLA Modules:
  0.0 60.2 jit_solution(18215430092541449158)
XLA Ops:
  0.0 20.2 %shard_map.55 = (bf16[16,32,1024]{2,1,0:T(8,128)(2,1)}, bf16[4,2,8,1024]{3,2,1,0:T(8,128)(2,1)}, s32[4,2,1024]{2,1,0:T(2,128)}) custom-call(bf16[32,4096]{1,0:T(8,128)(2,1)} %orb_hbm.1, bf16[2,8,1024]{2,1,0:T(8,128)(2,1)} %bitcast.6, s32[2,1024]{1,0:T(2,128)} %pair_ref.1), custom_call_target="tpu_custom_call" | custom-call | tf_op jit(solution)/shard_map/pallas_call | solution.py:169
  20.3 12.8 %shard_map.56 = (bf16[4096,1024]{1,0:T(8,128)(2,1)}, f32[16,1024]{1,0:T(8,128)}) custom-call(s32[4,2,1024]{2,1,0:T(2,128)} %get-tuple-element.10.pair_ref, bf16[4,16,1024]{2,1,0:T(8,128)(2,1)} %bitcast.5, bf16[512,1024]{1,0:T(8,128)(2,1)} %bitcast.4), custom_call_target="tpu_custom_call" | custom-call | tf_op jit(solution)/shard_map/pallas_call | solution.py:241
  33.1 0.0 copy-start
  33.1 25.4 %shard_map.57 = bf16[8,16,1024]{2,1,0:T(8,128)(2,1)} custom-call(f32[16,1024]{1,0:T(8,128)} %get-tuple-element.13.field_ref, f32[1,1024]{1,0:T(1,128)} %bitcast.7, bf16[1024,4096]{1,0:T(8,128)(2,1)} %eig_ref.1, bf16[4096,1024]{1,0:T(8,128)(2,1)} %get-tuple-element.14.dens_ref), custom_call_target="tpu_custom_call" | custom-call | tf_op jit(solution)/shard_map/pallas_call | solution.py:427
  58.5 0.0 copy-done
  58.5 1.6 %select_reduce_fusion = f32[16,1024]{1,0:T(8,128)} fusion(bf16[8,16,1024]{2,1,0:T(8,128)(2,1)} %shard_map.57, pred[1024]{0:T(1024)(128)(4,1)S(1)} %compare_reduce_fusion), kind=kLoop, calls=%fused_computation | loop fusion | flops 376832 | bytes 328704 | tf_op jit(solution)/shard_map/reduce_sum | solution.py:458
  (1 shorter events, 0.0 us)
Async XLA Ops:
  33.1 25.4 %copy-start = (s32[2,1024]{1,0:T(2,128)S(1)}, s32[2,1024]{1,0:T(2,128)}, u32[]{:S(2)}) copy-start(s32[2,1024]{1,0:T(2,128)} %pair_ref.1) | copy-start | bytes 24580

commit v6 on v4

--- a/solution.py
+++ b/solution.py
@@ -197,8 +197,14 @@
     def block_index(b):
         return pair_ref[b // steps, :, columns(lax.rem(b, steps), block)]
 
-    def write_out(b):
-        return pltpu.make_async_copy(blocks.at[b], dens_ref.at[:, columns(b, block)], sems.at[b])
+    step = min(512, width)
+    chunks = width // step
+
+    def write_out(b, c):
+        rows = pl.ds(c * step, step)
+        return pltpu.make_async_copy(
+            blocks.at[b, rows], dens_ref.at[rows, columns(b, block)], sems.at[b * chunks + c]
+        )
 
     @pl.loop(0, count)
     def _(b):
@@ -213,24 +219,24 @@
 
             left, right = pick(0), pick(1)
             trial = trial_ref[b // steps, :, columns(lax.rem(b, steps), block)]
-            step = min(512, width)
-            for c in range(width // step):
+            for c in range(chunks):
                 rows = pl.ds(c * step, step)
                 part = turned[rows, :]
                 one = jnp.dot(part, left, preferred_element_type=jnp.float32)
                 two = jnp.dot(part, right, preferred_element_type=jnp.float32)
                 dens = (one * two).astype(jnp.bfloat16)
                 blocks[b, rows, :] = dens
+                write_out(b, c).start()
                 field_ref[:, rows] += lax.dot_general(
                     trial, dens, (((1,), (1,)), ((), ())), preferred_element_type=jnp.float32
                 )
-            write_out(b).start()
 
     @pl.loop(0, count)
     def _(b):
         @pl.when(jnp.max(block_index(b)) >= 0)
         def _():
-            write_out(b).wait()
+            for c in range(chunks):
+                write_out(b, c).wait()
 
 
 def densities(pairs, trials, table):
@@ -250,7 +256,7 @@
         scratch_shapes=[
             pltpu.VMEM((width, orbs), jnp.bfloat16),
             pltpu.VMEM((blocks, width, block), jnp.bfloat16),
-            pltpu.SemaphoreType.DMA((blocks,)),
+            pltpu.SemaphoreType.DMA((blocks * (width // min(512, width)),)),
         ],
     )(pairs, trials, table.reshape(orbs, width))
 
@@ -305,9 +311,6 @@
         )
         for g in range(groups)
     ]
-    for copy in dens_loads:
-        copy.start()
-
     def remote(src, dst, send, recv, target):
         return pltpu.make_async_remote_copy(
             src_ref=src, dst_ref=dst, send_sem=send, recv_sem=recv,
@@ -322,6 +325,8 @@
 
     field = split_rows(field_ref[...])
     load.wait()
+    for copy in dens_loads:
+        copy.start()
     for c in range(eig.shape[0] // LANES):
         part = fold(
             lax.dot_general(
@@ -445,15 +450,16 @@
         ],
         compiler_params=pltpu.CompilerParams(collective_id=1, has_side_effects=True),
     )(field, screening.reshape(1, neig), eigenpotentials, dens)
-    return jnp.sum(parts.astype(f32), 0)
+    return parts
 
 
 def shards(count, slabs, orbitals, eigenpotentials, screening, trial_vectors, pair_index):
     table, trials, pairs = spread(count, slabs, orbitals, trial_vectors, pair_index)
     dens, field = densities(pairs, trials, table)
     slots = trial_vectors.shape[1]
-    direct = apply_direct(count, slabs, field, screening, eigenpotentials, dens, slots)
-    return jnp.where(pair_index[:1] >= 0, direct, 0.0)
+    parts = apply_direct(count, slabs, field, screening, eigenpotentials, dens, slots)
+    is_live = pair_index[:1][None] >= 0
+    return jnp.sum(jnp.where(is_live, parts.astype(jnp.float32), 0.0), 0)
 
 
 def solution(mesh):

time: 61.2 us -> 60 us (0.980)
  Pallas kernels: 59.6 us -> 58 us
    pallas_call x1, Pallas kernels: 14.2 us -> 12.6 us  [densities(): pl.pallas_call(density_kernel, out_shape=(jax.ShapeDtypeStruct((width, gr...]
    reduce_sum x1, other arithmetic: 1 us -> 1.64 us  [shards(): return jnp.sum(jnp.where(is_live, parts.astype(jnp.float32), 0.0), 0)]
    select_n x1 -> x0, other arithmetic: 0.64 us -> none  [shards(): return jnp.where(pair_index[:1] >= 0, direct, 0.0)]
where the time goes in v6:
time: 60 us; the launch traced here: 59.7 us
  Pallas kernels  58 us (97%)
  other arithmetic  1.67 us (3%)
    pallas_call x1, Pallas kernels, apply_direct(): pl.pallas_call(functools.partial(apply_kernel, count, slabs), out_shape=j...  25.1 us
    pallas_call x1, Pallas kernels, spread(): pl.pallas_call(functools.partial(spread_kernel, groups, slabs), out_shape...  20.2 us
    pallas_call x1, Pallas kernels, densities(): pl.pallas_call(density_kernel, out_shape=(jax.ShapeDtypeStruct((width, gr...  12.6 us
    reduce_sum x1, other arithmetic, shards(): return jnp.sum(jnp.where(is_live, parts.astype(jnp.float32), 0.0), 0)  1.64 us

profile of v6, /device:TPU:0, one launch (start us, length us, event | category | flops | bytes accessed | tf_op | source)
XLA Modules:
  0.0 59.7 jit_solution(12281394511593807696)
XLA Ops:
  0.0 20.2 %shard_map.55 = (bf16[16,32,1024]{2,1,0:T(8,128)(2,1)}, bf16[4,2,8,1024]{3,2,1,0:T(8,128)(2,1)}, s32[4,2,1024]{2,1,0:T(2,128)}) custom-call(bf16[32,4096]{1,0:T(8,128)(2,1)} %orb_hbm.1, bf16[2,8,1024]{2,1,0:T(8,128)(2,1)} %bitcast.6, s32[2,1024]{1,0:T(2,128)} %pair_ref.1), custom_call_target="tpu_custom_call" | custom-call | tf_op jit(solution)/shard_map/pallas_call | solution.py:169
  20.3 12.6 %shard_map.56 = (bf16[1024,4096]{1,0:T(8,128)(2,1)}, f32[16,1024]{1,0:T(8,128)}) custom-call(s32[4,2,1024]{2,1,0:T(2,128)} %get-tuple-element.10.pair_ref, bf16[4,16,1024]{2,1,0:T(8,128)(2,1)} %bitcast.5, bf16[512,1024]{1,0:T(8,128)(2,1)} %bitcast.4), custom_call_target="tpu_custom_call" | custom-call | tf_op jit(solution)/shard_map/pallas_call | solution.py:248
  32.9 0.0 copy-start
  32.9 25.1 %shard_map.57 = bf16[8,16,1024]{2,1,0:T(8,128)(2,1)} custom-call(f32[16,1024]{1,0:T(8,128)} %get-tuple-element.13.field_ref, f32[1,1024]{1,0:T(1,128)} %bitcast.7, bf16[1024,4096]{1,0:T(8,128)(2,1)} %eig_ref.1, bf16[1024,4096]{1,0:T(8,128)(2,1)} %get-tuple-element.14.dens_ref), custom_call_target="tpu_custom_call" | custom-call | tf_op jit(solution)/shard_map/pallas_call | solution.py:431
  58.0 0.0 copy-done
  58.1 1.6 %select_reduce_fusion = f32[16,1024]{1,0:T(8,128)} fusion(bf16[8,16,1024]{2,1,0:T(8,128)(2,1)} %shard_map.57, pred[1024]{0:T(1024)(128)(4,1)S(1)} %compare_reduce_fusion), kind=kLoop, calls=%fused_computation | loop fusion | flops 376832 | bytes 328704 | tf_op jit(solution)/shard_map/reduce_sum | solution.py:462
  (1 shorter events, 0.0 us)
Async XLA Ops:
  32.9 25.2 %copy-start = (s32[2,1024]{1,0:T(2,128)S(1)}, s32[2,1024]{1,0:T(2,128)}, u32[]{:S(2)}) copy-start(s32[2,1024]{1,0:T(2,128)} %pair_ref.1) | copy-start | bytes 24580

commit v7 on v4

--- a/solution.py
+++ b/solution.py
@@ -385,9 +385,9 @@
         copy.wait()
 
     def apply_to(g):
-        @pl.loop(0, slots // 256)
+        @pl.loop(0, slots // 512)
         def _(c):
-            cols = columns(c, 256)
+            cols = columns(c, 512)
             shares[g, :, cols] = fold(
                 jnp.dot(potential[...], dens[g, :, cols], preferred_element_type=jnp.float32)
             ).astype(shares.dtype)

time: 61.2 us -> 60.1 us (0.982); the launches traced: 61.3 us -> 59.4 us
  Pallas kernels: 59.6 us -> 57.7 us
    pallas_call x1, Pallas kernels: 14.2 us -> 12.5 us  [densities(): pl.pallas_call(density_kernel, out_shape=(jax.ShapeDtypeStruct((width, gr...]
where the time goes in v7:
time: 60.1 us; the launch traced here: 59.4 us
  Pallas kernels  57.7 us (96%)
  other arithmetic  1.66 us (3%)
    pallas_call x1, Pallas kernels, apply_direct(): pl.pallas_call(functools.partial(apply_kernel, count, slabs), out_shape=j...  24.9 us
    pallas_call x1, Pallas kernels, spread(): pl.pallas_call(functools.partial(spread_kernel, groups, slabs), out_shape...  20.2 us
    pallas_call x1, Pallas kernels, densities(): pl.pallas_call(density_kernel, out_shape=(jax.ShapeDtypeStruct((width, gr...  12.5 us

profile of v7, /device:TPU:0, one launch (start us, length us, event | category | flops | bytes accessed | tf_op | source)
XLA Modules:
  0.0 59.4 jit_solution(9295831974375737802)
XLA Ops:
  0.0 20.2 %shard_map.55 = (bf16[16,32,1024]{2,1,0:T(8,128)(2,1)}, bf16[4,2,8,1024]{3,2,1,0:T(8,128)(2,1)}, s32[4,2,1024]{2,1,0:T(2,128)}) custom-call(bf16[32,4096]{1,0:T(8,128)(2,1)} %orb_hbm.1, bf16[2,8,1024]{2,1,0:T(8,128)(2,1)} %bitcast.6, s32[2,1024]{1,0:T(2,128)} %pair_ref.1), custom_call_target="tpu_custom_call" | custom-call | tf_op jit(solution)/shard_map/pallas_call | solution.py:169
  20.3 12.5 %shard_map.56 = (bf16[1024,4096]{1,0:T(8,128)(2,1)}, f32[16,1024]{1,0:T(8,128)}) custom-call(s32[4,2,1024]{2,1,0:T(2,128)} %get-tuple-element.10.pair_ref, bf16[4,16,1024]{2,1,0:T(8,128)(2,1)} %bitcast.5, bf16[512,1024]{1,0:T(8,128)(2,1)} %bitcast.4), custom_call_target="tpu_custom_call" | custom-call | tf_op jit(solution)/shard_map/pallas_call | solution.py:242
  32.8 0.0 copy-start
  32.8 24.9 %shard_map.57 = bf16[8,16,1024]{2,1,0:T(8,128)(2,1)} custom-call(f32[16,1024]{1,0:T(8,128)} %get-tuple-element.13.field_ref, f32[1,1024]{1,0:T(1,128)} %bitcast.7, bf16[1024,4096]{1,0:T(8,128)(2,1)} %eig_ref.1, bf16[1024,4096]{1,0:T(8,128)(2,1)} %get-tuple-element.14.dens_ref), custom_call_target="tpu_custom_call" | custom-call | tf_op jit(solution)/shard_map/pallas_call | solution.py:426
  57.7 1.0 %convert_reduce_fusion = f32[16,1024]{1,0:T(8,128)S(1)} fusion(bf16[8,16,1024]{2,1,0:T(8,128)(2,1)} %shard_map.57), kind=kLoop, calls=%fused_computation | loop fusion | flops 245760 | bytes 327680 | tf_op jit(solution)/shard_map/reduce_sum | solution.py:448
  58.7 0.0 copy-done
  58.7 0.6 %broadcast_select_fusion = f32[16,1024]{1,0:T(8,128)} fusion(f32[16,1024]{1,0:T(8,128)S(1)} %convert_reduce_fusion, pred[1024]{0:T(1024)(128)(4,1)S(1)} %compare_reduce_fusion), kind=kLoop, calls=%fused_computation.1 | loop fusion | flops 16384 | bytes 132096 | tf_op jit(solution)/shard_map/jit(_where)/select_n | solution.py:456
  (1 shorter events, 0.0 us)
Async XLA Ops:
  32.8 25.9 %copy-start = (s32[2,1024]{1,0:T(2,128)S(1)}, s32[2,1024]{1,0:T(2,128)}, u32[]{:S(2)}) copy-start(s32[2,1024]{1,0:T(2,128)} %pair_ref.1) | copy-start | bytes 24580
